TPU v7x, 32 devices: a whole 2x2x4 slice. The times are simulated.
32 devices in a mesh: groups: 2 (over y), samples: 8 (over z, x), genome: 2 (over core).
Axes of the slice: x: 2, y: 2, z: 4, core: 2. Of those that a mesh axis runs over, the one named last changes fastest.
Arguments:
- genotypes: bfloat16 [16384, 1536], P(('groups', 'samples'), 'genome'), parts along dimension 0, may hold values from 0 to 2
- chromosome: int32 [3072], P('groups'), parts along dimension 0, may hold values from 1 to 3, as said below
- blocks: int32 [3072], P('groups'), parts along dimension 0, may hold values from 0 to 199, never falling along the last dimension, each value on 1 to 16 neighbouring positions
- annotation: int32 [97, 3072], P(None, 'groups'), parts along dimension 1, may hold values 0 or 1
- reach: int32 [3072], P('groups'), parts along dimension 0, may hold values from 384 to 768
Outputs:
- ld_scores: float32 [97, 3072], P(None, ('groups', 'genome')), parts along dimension 1
- block_sums: float32 [97, 400], P(None, 'groups'), parts along dimension 1
There are 2 independent parts, one for each index of `groups`. A program takes and returns all parts, laid end to end along the dimension named above; each array names one. Nothing has to cross between parts.
Inputs may be any that keep to these rules, and one draw needn't show every extreme that they name: chromosome ids never fall along the window and rise by one at each of 2 boundaries.
All inputs are finite; a program needn't handle non-finite values.
Results may differ from a plain program's by a relative error of at most 0.0015.
Values may be sent and summed in bfloat16 or wider, within the bound.
No kernel may reach another device: no remote copies, remote signals or barrier semaphores. Data moves between devices by JAX's collectives and lax.ppermute only.
A program may use at most 64 MiB of HBM per device.

v0:
```python
import jax
import jax.numpy as jnp
from jax import lax
from jax.sharding import PartitionSpec as P

BAND = 768
NBLK = 200
VAR_EPS = 1e-06


def shifted(block, axis, distance):
    devices = range(lax.axis_size(axis))
    route = [(i - distance, i) for i in devices if i - distance in devices]
    return lax.ppermute(block, axis, route)


def shear_band(product, band_len):
    rows_here, columns = product.shape
    flattened = jnp.pad(product.reshape(-1), (0, rows_here))
    return flattened.reshape(rows_here, columns + 1)[:, :band_len]


def unshear_band(gram_band):
    rows_here, band_len = gram_band.shape
    col_span = rows_here + band_len
    padded = jnp.pad(gram_band, ((0, 0), (1, rows_here)))
    return padded.reshape(-1)[: rows_here * col_span].reshape(rows_here, col_span)


def gram_rows(extended, row_start, row_count, band_len):
    left_cols = lax.dynamic_slice_in_dim(extended, row_start, row_count, 1)
    right_cols = lax.dynamic_slice_in_dim(extended, row_start + 1, row_count + band_len - 1, 1)
    product = lax.dot_general(
        left_cols, right_cols, (((0,), (0,)), ((), ())), preferred_element_type=jnp.float32
    )
    return shear_band(product, band_len)


def score_terms(
    gram_band,
    row_start,
    col_means,
    scales,
    chrom_ext,
    reach_own,
    annot_ext,
    first_col,
    snp_total,
    samples_all,
):
    row_count, band_len = gram_band.shape
    col_span = row_count + band_len
    dense_band = unshear_band(gram_band)
    mean_rows = lax.dynamic_slice_in_dim(col_means, row_start, row_count)
    scale_rows = lax.dynamic_slice_in_dim(scales, row_start, row_count)
    chrom_rows = lax.dynamic_slice_in_dim(chrom_ext, row_start, row_count)
    correl = (dense_band / samples_all - mean_rows[:, None] * col_means[None, :]) / (
        scale_rows[:, None] * scales[None, :]
    )
    squared = correl * correl
    unbiased = squared - (1.0 - squared) / (samples_all - 2.0)
    offsets = jnp.arange(col_span)[None, :] - jnp.arange(row_count)[:, None]
    col_index = first_col + row_start + jnp.arange(col_span)
    allowed = (
        (offsets >= 1)
        & (offsets <= reach_own[:, None])
        & (col_index[None, :] < snp_total)
        & (chrom_rows[:, None] == chrom_ext[None, :])
    )
    weights = jnp.where(allowed, unbiased, 0.0)
    annot_rows = lax.dynamic_slice_in_dim(annot_ext, row_start, row_count, 1)
    forward = lax.dot_general(
        annot_ext, weights, (((1,), (1,)), ((), ())), precision=lax.Precision.HIGHEST
    )
    backward = jnp.dot(annot_rows, weights, precision=lax.Precision.HIGHEST)
    empty_scores = jnp.zeros(annot_ext.shape, jnp.float32)
    placed_fore = lax.dynamic_update_slice_in_dim(empty_scores, forward, row_start, 1)
    return backward + placed_fore


def body(genotypes, chromosome, blocks, annotation, reach):
    slab_len = genotypes.shape[1]
    band_len = BAND
    snp_total = chromosome.shape[0]
    samples_all = float(genotypes.shape[0] * lax.axis_size("samples"))
    first_col = lax.axis_index("genome") * slab_len
    next_cols = shifted(genotypes, "genome", -1)
    extended = jnp.concatenate([genotypes, next_cols], axis=1)
    ext_values = extended.astype(jnp.float32)
    col_sums, squares = lax.psum(
        (jnp.sum(ext_values, 0), jnp.sum(ext_values * ext_values, 0)), "samples"
    )
    col_means = col_sums / samples_all
    variance = squares / samples_all - col_means * col_means + VAR_EPS
    scales = jnp.sqrt(variance)
    chrom_pad = jnp.pad(chromosome, (0, band_len), constant_values=-1)
    chrom_ext = lax.dynamic_slice_in_dim(chrom_pad, first_col, slab_len + band_len)
    reach_own = lax.dynamic_slice_in_dim(reach, first_col, slab_len)
    annot_pad = jnp.pad(annotation.astype(jnp.float32), ((0, 0), (0, band_len)))
    annot_ext = lax.dynamic_slice_in_dim(annot_pad, first_col, slab_len + band_len, 1)
    gram_band = lax.psum(gram_rows(extended, 0, slab_len, band_len), "samples")
    scores = score_terms(
        gram_band,
        0,
        col_means,
        scales,
        chrom_ext,
        reach_own,
        annot_ext,
        first_col,
        snp_total,
        samples_all,
    )
    carried = shifted(scores[:, slab_len:].astype(jnp.bfloat16), "genome", 1).astype(jnp.float32)
    ld_scores = annot_ext[:, :slab_len] + scores[:, :slab_len] + carried
    block_own = lax.dynamic_slice_in_dim(blocks, first_col, slab_len)
    onehot = (block_own[None, :] == jnp.arange(NBLK)[:, None]).astype(jnp.float32)
    block_part = lax.dot_general(
        ld_scores, onehot, (((1,), (1,)), ((), ())), precision=lax.Precision.HIGHEST
    )
    block_sums = lax.psum(block_part, "genome")
    return (ld_scores, block_sums)


def solution(mesh):
    placed = (
        P(("groups", "samples"), "genome"),
        P("groups"),
        P("groups"),
        P(None, "groups"),
        P("groups"),
    )
    return jax.shard_map(
        body,
        mesh=mesh,
        in_specs=placed,
        out_specs=(P(None, ("groups", "genome")), P(None, "groups")),
        check_vma=False,
    )
```

profile of v0, /device:TPU:0, one launch (start us, length us, event | category | flops | bytes accessed | tf_op | source)
XLA Modules:
  0.0 224.0 jit_solution(105049170321501688)
XLA Ops:
  7.2 1.4 collective-permute-start
  8.7 1.5 constant_dynamic-update-slice_fusion.1
  10.2 2.7 %collective-permute-done = bf16[1024,768]{1,0:T(8,128)(2,1)S(1)} collective-permute-done((bf16[1024,768]{1,0:T(8,128)(2,1)}, bf16[1024,768]{1,0:T(8,128)(2,1)S(1)}, u32[]{:S(2)}, u32[]{:S(2)}) %collective-permute-start) | collective-permute-done | bytes 1572896 | tf_op jit(solution)/shard_map/ppermute | solution.py:14
  13.0 1.6 copy-done
  14.6 4.9 %convolution_bitcast_fusion = f32[768,1535]{0,1:T(8,128)} fusion(bf16[1024,768]{1,0:T(8,128)(2,1)S(1)} %copy-done.1, bf16[1024,1536]{1,0:T(8,128)(2,1)S(1)} %constant_dynamic-update-slice_fusion), kind=kOutput, calls=%fused_computation.11 | convolution fusion | flops 2414346240 | bytes 9434112 | tf_op jit(solution)/shard_map/dot_general | solution.py:33
  19.6 6.1 %copy.7 = f32[768,1535]{1,0:T(8,128)} copy(f32[768,1535]{0,1:T(8,128)} %convolution_bitcast_fusion) | data formatting | bytes 9431040 | tf_op jit(solution)/shard_map/dot_general | solution.py:33
  25.6 7.8 %reshape.30 = f32[1178880]{0:T(1024)} reshape(f32[768,1535]{1,0:T(8,128)} %copy.7) | data formatting | bytes 9431040 | tf_op jit(solution)/shard_map/reshape | solution.py:19
  33.5 4.1 %pad.19 = f32[1179648]{0:T(1024)} pad(f32[1178880]{0:T(1024)} %reshape.30, f32[]{:T(128)} %constant.12.clone.1), padding=0_768 | pad | bytes 9434116 | tf_op jit(solution)/shard_map/jit(_pad)/pad | solution.py:19
  37.6 5.8 %reshape.31 = f32[768,1536]{1,0:T(8,128)} reshape(f32[1179648]{0:T(1024)} %pad.19) | data formatting | bytes 9437184 | tf_op jit(solution)/shard_map/reshape | solution.py:20
  43.4 3.3 %slice.21 = f32[768,768]{1,0:T(8,128)} slice(f32[768,1536]{1,0:T(8,128)} %reshape.31), slice={[0:768], [0:768]} | slice | bytes 4718592 | tf_op jit(solution)/shard_map/slice | solution.py:20
  47.1 2.8 %convert_reduce_fusion = (f32[1536]{0:T(1024)S(1)}, f32[1536]{0:T(1024)S(1)}) fusion(bf16[1024,1536]{1,0:T(8,128)(2,1)} %copy-done), kind=kLoop, calls=%fused_computation.1 | loop fusion | flops 6288384 | bytes 3158016 | tf_op jit(solution)/shard_map/reduce_sum | solution.py:91
  49.9 40.4 %all-reduce.5 = (f32[1536]{0:T(1024)S(1)}, f32[1536]{0:T(1024)S(1)}) all-reduce(f32[1536]{0:T(1024)S(1)} %get-tuple-element.3, f32[1536]{0:T(1024)S(1)} %get-tuple-element.2), channel_id=1, replica_groups=mesh['groups'=2,'samples'=8,'genome'=2] {'samples'}, use_global_device_ids=true, to_apply=%region_4.5 | all-reduce | flops 3072 | bytes 24576 | tf_op jit(solution)/shard_map/psum | solution.py:90
  90.2 68.6 %all-reduce.9.cloned.1.call-done = f32[768,768]{1,0:T(8,128)} async-done(((f32[768,768]{1,0:T(8,128)}), f32[768,768]{1,0:T(8,128)}) %all-reduce.9.cloned.1.call-update) | async-done | bytes 2359312 | tf_op jit(solution)/shard_map/psum | solution.py:101
  158.9 4.8 %pad.20 = f32[768,1537]{1,0:T(8,128)} pad(f32[768,768]{1,0:T(8,128)} %all-reduce.9.cloned.1.call-done, f32[]{:T(128)} %constant.12.clone.1), padding=0_0x1_768 | pad | bytes 7080964 | tf_op jit(solution)/shard_map/jit(_pad)/pad | solution.py:26
  163.7 8.1 %reshape.32 = f32[1180416]{0:T(1024)} reshape(f32[768,1537]{1,0:T(8,128)} %pad.20) | data formatting | bytes 9443328 | tf_op jit(solution)/shard_map/reshape | solution.py:27
  171.8 3.9 %slice_multiply_fusion = f32[1179648]{0:T(1024)} fusion(f32[1180416]{0:T(1024)} %reshape.32), kind=kLoop, calls=%fused_computation.3 | loop fusion | flops 1179648 | bytes 9437184 | tf_op jit(solution)/shard_map/div | solution.py:57
  175.8 5.8 %div.25 = f32[768,1536]{1,0:T(8,128)} reshape(f32[1179648]{0:T(1024)} %slice_multiply_fusion) | data formatting | bytes 9437184 | tf_op jit(solution)/shard_map/div | solution.py:57
  181.6 5.4 %subtract_select_fusion = f32[768,1536]{1,0:T(8,128)S(1)} fusion(f32[768,1536]{1,0:T(8,128)} %div.25, f32[1536]{0:T(1024)S(1)} %get-tuple-element.7, f32[768]{0:T(1024)S(1)} %dynamic_slice.35, f32[1536]{0:T(1024)S(1)} %get-tuple-element.6, f32[768]{0:T(1024)S(1)} %dynamic_slice.34, s32[1536]{0:T(1024)S(1)} %pad_dynamic-slice_fusion.5, ...), kind=kLoop, calls=%fused_computation.4 | loop fusion | flops 18874368 | bytes 9469440 | tf_op jit(solution)/shard_map/jit(_where)/select_n | solution.py:70
  187.0 4.7 %fusion.7 = f32[97,768]{1,0:T(8,128)S(1)} fusion(f32[768,1536]{1,0:T(8,128)S(1)} %subtract_select_fusion, s32[]{:T(128)S(6)} %select_n.12, f32[97,1536]{1,0:T(8,128)S(1)} %convert_element_type.17), kind=kOutput, calls=%fused_computation.16 | convolution fusion | flops 1373110272 | bytes 5612548 | tf_op jit(solution)/shard_map/dot_general | solution.py:72
  191.7 2.7 %convolution_add_fusion = f32[97,1536]{1,0:T(8,128)S(1)} fusion(f32[768,1536]{1,0:T(8,128)S(1)} %subtract_select_fusion, f32[97,768]{1,0:T(8,128)S(1)} %fusion.7, s32[]{:T(128)S(6)} %select_n.12, f32[97,1536]{1,0:T(8,128)S(1)} %convert_element_type.17), kind=kOutput, calls=%fused_computation.13 | convolution fusion | flops 1373259264 | bytes 6208516 | tf_op jit(solution)/shard_map/dot_general | solution.py:75
  194.5 1.3 collective-permute-start.1
  196.9 1.1 fusion.8
  198.0 17.6 %all-reduce.11.cloned.1.call-done = f32[97,200]{0,1:T(8,128)} async-done(((f32[97,200]{0,1:T(8,128)}), f32[97,200]{0,1:T(8,128)}) %all-reduce.11.cloned.1.call-update) | async-done | bytes 77616 | tf_op jit(solution)/shard_map/psum | solution.py:121
  215.6 1.5 copy.11
  (30 shorter events, 1.6 us)
Async XLA Ops:
  7.2 7.5 %copy-start.1 = (bf16[1024,768]{1,0:T(8,128)(2,1)S(1)}, bf16[1024,768]{1,0:T(8,128)(2,1)}, u32[]{:S(2)}) copy-start(bf16[1024,768]{1,0:T(8,128)(2,1)} %param.5) | copy-start | bytes 4718596
  7.2 151.7 %all-reduce.9.cloned.1.call-start = ((), (), s32[]{:S(2)}) async-start(), calls=%async_computation | async-start | bytes 4718592 | tf_op jit(solution)/shard_map/psum | solution.py:101
  7.2 5.6 %collective-permute-start = (bf16[1024,768]{1,0:T(8,128)(2,1)}, bf16[1024,768]{1,0:T(8,128)(2,1)S(1)}, u32[]{:S(2)}, u32[]{:S(2)}) collective-permute-start(bf16[1024,768]{1,0:T(8,128)(2,1)} %param.5), channel_id=1, source_target_pairs={{1,0},{3,2},{5,4},{7,6},{9,8},{11,10},{13,12},{15,14},{17,16},{19,... | collective-permute-start | bytes 4718600 | tf_op jit(solution)/shard_map/ppermute | solution.py:14
  13.0 1.6 copy-start
  43.4 3.4 %copy-start.3 = (s32[97,1536]{1,0:T(8,128)S(1)}, s32[97,1536]{1,0:T(8,128)}, u32[]{:S(2)}) copy-start(s32[97,1536]{1,0:T(8,128)} %param.8) | copy-start | bytes 1787908
  43.4 3.5 %copy-start.5 = (s32[1536]{0:T(1024)S(1)}, s32[1536]{0:T(1024)}, u32[]{:S(2)}) copy-start(s32[1536]{0:T(1024)} %param.9) | copy-start | bytes 18436
  43.4 3.6 %copy-start.4 = (s32[1536]{0:T(1024)S(1)}, s32[1536]{0:T(1024)}, u32[]{:S(2)}) copy-start(s32[1536]{0:T(1024)} %param.6) | copy-start | bytes 18436
  46.7 168.9 %all-reduce.11.cloned.1.call-start = ((), (), s32[]{:S(2)}) async-start(), calls=%async_computation.1 | async-start | bytes 204800 | tf_op jit(solution)/shard_map/psum | solution.py:121
  191.7 4.1 %copy-start.6 = (s32[1536]{0:T(1024)S(1)}, s32[1536]{0:T(1024)}, u32[]{:S(2)}) copy-start(s32[1536]{0:T(1024)} %param.7) | copy-start | bytes 18436
  194.5 2.3 %collective-permute-start.1 = (bf16[97,768]{1,0:T(8,128)(2,1)S(1)}, bf16[97,768]{1,0:T(8,128)(2,1)S(1)}, u32[]{:S(2)}, u32[]{:S(2)}) collective-permute-start(bf16[97,768]{1,0:T(8,128)(2,1)S(1)} %slice.30), channel_id=1, source_target_pairs={{0,1},{2,3},{4,5},{6,7},{8,9},{10,11},{12,13},{14,15},{16,17},{18,... | collective-permute-start | bytes 446984 | tf_op jit(solution)/shard_map/ppermute | solution.py:14
  196.9 20.3 %copy-start.2 = (f32[97,768]{1,0:T(8,128)}, f32[97,768]{1,0:T(8,128)S(1)}, u32[]{:S(2)}) copy-start(f32[97,768]{1,0:T(8,128)S(1)} %fusion.9) | copy-start | bytes 893956
Sparse Core Ops, SparseCore 0:
  46.8 112.0 all-reduce.8
  198.1 17.4 all-reduce.10
where the time goes:
time: 225 us; the launch traced here: 224 us
  waiting for transfers between devices  89.8 us (40%)
  local copies, waits for them, and re-layouts  51 us (23%)
  blocking collectives  40.4 us (18%)
  between operations  14.2 us (6%)
  matrix products  13.5 us (6%)
  other arithmetic  12.3 us (5%)
  starting transfers between devices  2.8 us (1%)
    psum x1, waiting for transfers between devices, body(): gram_band = lax.psum(gram_rows(extended, 0, slab_len, band_len), 'samples')  68.6 us
    psum x1, blocking collectives, body(): lax.psum((jnp.sum(ext_values, 0), jnp.sum(ext_values * ext_values, 0)), '...  40.4 us
    psum x1, waiting for transfers between devices, body(): block_sums = lax.psum(block_part, 'genome')  17.6 us
    reshape x1, local copies, waits for them, and re-layouts, unshear_band(): padded.reshape(-1)[:rows_here * col_span].reshape(rows_here, col_span)  8.14 us
    reshape x1, local copies, waits for them, and re-layouts, shear_band(): flattened = jnp.pad(product.reshape(-1), (0, rows_here))  7.84 us
    dot_general x1, local copies, waits for them, and re-layouts, gram_rows(): lax.dot_general(left_cols, right_cols, (((0,), (0,)), ((), ())), preferre...  6.05 us
    reshape x1, local copies, waits for them, and re-layouts, shear_band(): return flattened.reshape(rows_here, columns + 1)[:, :band_len]  5.81 us
    div x1, local copies, waits for them, and re-layouts, score_terms(): dense_band / samples_all - mean_rows[:, None] * col_means[None, :]  5.81 us
  transfers between devices with their start and end apart: 4, of which 4 were waited for; matrix products, arithmetic and copies ran while one was open for 2% of the time, Pallas kernels for 0%

commit v1 on v0

--- a/solution.py
+++ b/solution.py
@@ -118,7 +118,7 @@
     block_part = lax.dot_general(
         ld_scores, onehot, (((1,), (1,)), ((), ())), precision=lax.Precision.HIGHEST
     )
-    block_sums = lax.psum(block_part, "genome")
+    block_sums = jnp.sum(lax.all_gather(block_part, "genome"), axis=0)
     return (ld_scores, block_sums)
 
 

time: 225 us -> 208 us (0.924)
  waiting for transfers between devices: 89.8 us -> 72.3 us
    psum x1 -> x0, waiting for transfers between devices: 17.6 us -> none  [body(): block_sums = lax.psum(block_part, 'genome')]
    unnamed x16 -> x15, local copies, waits for them, and re-layouts: 4.72 us -> 3.18 us
  transfers between devices with their start and end apart: 4 -> 3, of which waited for: 4 -> 3; matrix products, arithmetic and copies ran while one was open for 2% -> 2% of each run, Pallas kernels for 0% -> 0%
where the time goes in v1:
time: 208 us; the launch traced here: 207 us
  waiting for transfers between devices  72.3 us (35%)
  local copies, waits for them, and re-layouts  49.5 us (24%)
  blocking collectives  42.3 us (20%)
  between operations  14.2 us (7%)
  other arithmetic  12.9 us (6%)
  matrix products  12.8 us (6%)
  starting transfers between devices  2.76 us (1%)
    psum x1, waiting for transfers between devices, body(): gram_band = lax.psum(gram_rows(extended, 0, slab_len, band_len), 'samples')  68.7 us
    psum x1, blocking collectives, body(): lax.psum((jnp.sum(ext_values, 0), jnp.sum(ext_values * ext_values, 0)), '...  40.4 us
    reshape x1, local copies, waits for them, and re-layouts, unshear_band(): padded.reshape(-1)[:rows_here * col_span].reshape(rows_here, col_span)  8.14 us
    reshape x1, local copies, waits for them, and re-layouts, shear_band(): flattened = jnp.pad(product.reshape(-1), (0, rows_here))  7.83 us
    dot_general x1, local copies, waits for them, and re-layouts, gram_rows(): lax.dot_general(left_cols, right_cols, (((0,), (0,)), ((), ())), preferre...  6.05 us
    reshape x1, local copies, waits for them, and re-layouts, shear_band(): return flattened.reshape(rows_here, columns + 1)[:, :band_len]  5.83 us
    div x1, local copies, waits for them, and re-layouts, score_terms(): dense_band / samples_all - mean_rows[:, None] * col_means[None, :]  5.83 us
    select_n x1, other arithmetic, score_terms(): weights = jnp.where(allowed, unbiased, 0.0)  5.45 us
  transfers between devices with their start and end apart: 3, of which 3 were waited for; matrix products, arithmetic and copies ran while one was open for 2% of the time, Pallas kernels for 0%

profile of v1, /device:TPU:0, one launch (start us, length us, event | category | flops | bytes accessed | tf_op | source)
XLA Modules:
  0.0 206.9 jit_solution(8248477015087986288)
XLA Ops:
  7.2 1.4 collective-permute-start
  8.7 1.5 constant_dynamic-update-slice_fusion.1
  10.2 2.7 %collective-permute-done = bf16[1024,768]{1,0:T(8,128)(2,1)S(1)} collective-permute-done((bf16[1024,768]{1,0:T(8,128)(2,1)}, bf16[1024,768]{1,0:T(8,128)(2,1)S(1)}, u32[]{:S(2)}, u32[]{:S(2)}) %collective-permute-start) | collective-permute-done | bytes 1572896 | tf_op jit(solution)/shard_map/ppermute | solution.py:14
  13.0 1.6 copy-done
  14.6 4.9 %convolution_bitcast_fusion = f32[768,1535]{0,1:T(8,128)} fusion(bf16[1024,768]{1,0:T(8,128)(2,1)S(1)} %copy-done.1, bf16[1024,1536]{1,0:T(8,128)(2,1)S(1)} %constant_dynamic-update-slice_fusion), kind=kOutput, calls=%fused_computation.11 | convolution fusion | flops 2414346240 | bytes 9434112 | tf_op jit(solution)/shard_map/dot_general | solution.py:33
  19.6 6.1 %copy.8 = f32[768,1535]{1,0:T(8,128)} copy(f32[768,1535]{0,1:T(8,128)} %convolution_bitcast_fusion) | data formatting | bytes 9431040 | tf_op jit(solution)/shard_map/dot_general | solution.py:33
  25.6 7.8 %reshape.30 = f32[1178880]{0:T(1024)} reshape(f32[768,1535]{1,0:T(8,128)} %copy.8) | data formatting | bytes 9431040 | tf_op jit(solution)/shard_map/reshape | solution.py:19
  33.5 4.1 %pad.19 = f32[1179648]{0:T(1024)} pad(f32[1178880]{0:T(1024)} %reshape.30, f32[]{:T(128)} %constant.12.clone.1), padding=0_768 | pad | bytes 9434116 | tf_op jit(solution)/shard_map/jit(_pad)/pad | solution.py:19
  37.6 5.8 %reshape.31 = f32[768,1536]{1,0:T(8,128)} reshape(f32[1179648]{0:T(1024)} %pad.19) | data formatting | bytes 9437184 | tf_op jit(solution)/shard_map/reshape | solution.py:20
  43.4 3.3 %slice.21 = f32[768,768]{1,0:T(8,128)} slice(f32[768,1536]{1,0:T(8,128)} %reshape.31), slice={[0:768], [0:768]} | slice | bytes 4718592 | tf_op jit(solution)/shard_map/slice | solution.py:20
  47.0 2.8 %convert_reduce_fusion = (f32[1536]{0:T(1024)S(1)}, f32[1536]{0:T(1024)S(1)}) fusion(bf16[1024,1536]{1,0:T(8,128)(2,1)} %copy-done), kind=kLoop, calls=%fused_computation.1 | loop fusion | flops 6288384 | bytes 3158016 | tf_op jit(solution)/shard_map/reduce_sum | solution.py:91
  49.8 40.4 %all-reduce.5 = (f32[1536]{0:T(1024)S(1)}, f32[1536]{0:T(1024)S(1)}) all-reduce(f32[1536]{0:T(1024)S(1)} %get-tuple-element.3, f32[1536]{0:T(1024)S(1)} %get-tuple-element.2), channel_id=1, replica_groups=mesh['groups'=2,'samples'=8,'genome'=2] {'samples'}, use_global_device_ids=true, to_apply=%region_4.5 | all-reduce | flops 3072 | bytes 24576 | tf_op jit(solution)/shard_map/psum | solution.py:90
  90.2 68.7 %all-reduce.8.cloned.1.call-done = f32[768,768]{1,0:T(8,128)} async-done(((f32[768,768]{1,0:T(8,128)}), f32[768,768]{1,0:T(8,128)}) %all-reduce.8.cloned.1.call-update) | async-done | bytes 2359312 | tf_op jit(solution)/shard_map/psum | solution.py:101
  158.9 4.8 %pad.20 = f32[768,1537]{1,0:T(8,128)} pad(f32[768,768]{1,0:T(8,128)} %all-reduce.8.cloned.1.call-done, f32[]{:T(128)} %constant.12.clone.1), padding=0_0x1_768 | pad | bytes 7080964 | tf_op jit(solution)/shard_map/jit(_pad)/pad | solution.py:26
  163.7 8.1 %reshape.32 = f32[1180416]{0:T(1024)} reshape(f32[768,1537]{1,0:T(8,128)} %pad.20) | data formatting | bytes 9443328 | tf_op jit(solution)/shard_map/reshape | solution.py:27
  171.8 3.9 %slice_multiply_fusion = f32[1179648]{0:T(1024)} fusion(f32[1180416]{0:T(1024)} %reshape.32), kind=kLoop, calls=%fused_computation.3 | loop fusion | flops 1179648 | bytes 9437184 | tf_op jit(solution)/shard_map/div | solution.py:57
  175.8 5.8 %div.25 = f32[768,1536]{1,0:T(8,128)} reshape(f32[1179648]{0:T(1024)} %slice_multiply_fusion) | data formatting | bytes 9437184 | tf_op jit(solution)/shard_map/div | solution.py:57
  181.6 5.4 %subtract_select_fusion = f32[768,1536]{1,0:T(8,128)S(1)} fusion(f32[768,1536]{1,0:T(8,128)} %div.25, f32[1536]{0:T(1024)S(1)} %get-tuple-element.7, f32[768]{0:T(1024)S(1)} %dynamic_slice.35, f32[1536]{0:T(1024)S(1)} %get-tuple-element.6, f32[768]{0:T(1024)S(1)} %dynamic_slice.34, s32[1536]{0:T(1024)S(1)} %pad_dynamic-slice_fusion.5, ...), kind=kLoop, calls=%fused_computation.4 | loop fusion | flops 18874368 | bytes 9469440 | tf_op jit(solution)/shard_map/jit(_where)/select_n | solution.py:70
  187.1 4.7 %fusion.7 = f32[97,768]{1,0:T(8,128)S(1)} fusion(f32[768,1536]{1,0:T(8,128)S(1)} %subtract_select_fusion, s32[]{:T(128)S(6)} %select_n.12, f32[97,1536]{1,0:T(8,128)S(1)} %convert_element_type.17), kind=kOutput, calls=%fused_computation.17 | convolution fusion | flops 1373110272 | bytes 5612548 | tf_op jit(solution)/shard_map/dot_general | solution.py:72
  191.8 2.7 %convolution_add_fusion = f32[97,1536]{1,0:T(8,128)S(1)} fusion(f32[768,1536]{1,0:T(8,128)S(1)} %subtract_select_fusion, f32[97,768]{1,0:T(8,128)S(1)} %fusion.7, s32[]{:T(128)S(6)} %select_n.12, f32[97,1536]{1,0:T(8,128)S(1)} %convert_element_type.17), kind=kOutput, calls=%fused_computation.13 | convolution fusion | flops 1373259264 | bytes 6208516 | tf_op jit(solution)/shard_map/dot_general | solution.py:75
  194.5 1.3 collective-permute-start.1
  195.9 0.9 collective-permute-done.1
  197.4 2.0 all-gather.1
  199.3 0.7 reduce_sum.29
  (28 shorter events, 1.1 us)
Async XLA Ops:
  7.2 7.5 %copy-start.1 = (bf16[1024,768]{1,0:T(8,128)(2,1)S(1)}, bf16[1024,768]{1,0:T(8,128)(2,1)}, u32[]{:S(2)}) copy-start(bf16[1024,768]{1,0:T(8,128)(2,1)} %param.5) | copy-start | bytes 4718596
  7.2 151.7 %all-reduce.8.cloned.1.call-start = ((), (), s32[]{:S(2)}) async-start(), calls=%async_computation | async-start | bytes 4718592 | tf_op jit(solution)/shard_map/psum | solution.py:101
  7.2 5.6 %collective-permute-start = (bf16[1024,768]{1,0:T(8,128)(2,1)}, bf16[1024,768]{1,0:T(8,128)(2,1)S(1)}, u32[]{:S(2)}, u32[]{:S(2)}) collective-permute-start(bf16[1024,768]{1,0:T(8,128)(2,1)} %param.5), channel_id=1, source_target_pairs={{1,0},{3,2},{5,4},{7,6},{9,8},{11,10},{13,12},{15,14},{17,16},{19,... | collective-permute-start | bytes 4718600 | tf_op jit(solution)/shard_map/ppermute | solution.py:14
  13.0 1.6 copy-start
  43.4 3.3 %copy-start.3 = (s32[97,1536]{1,0:T(8,128)S(1)}, s32[97,1536]{1,0:T(8,128)}, u32[]{:S(2)}) copy-start(s32[97,1536]{1,0:T(8,128)} %param.8) | copy-start | bytes 1787908
  43.4 3.4 %copy-start.5 = (s32[1536]{0:T(1024)S(1)}, s32[1536]{0:T(1024)}, u32[]{:S(2)}) copy-start(s32[1536]{0:T(1024)} %param.9) | copy-start | bytes 18436
  43.4 3.5 %copy-start.4 = (s32[1536]{0:T(1024)S(1)}, s32[1536]{0:T(1024)}, u32[]{:S(2)}) copy-start(s32[1536]{0:T(1024)} %param.6) | copy-start | bytes 18436
  191.8 4.1 %copy-start.6 = (s32[1536]{0:T(1024)S(1)}, s32[1536]{0:T(1024)}, u32[]{:S(2)}) copy-start(s32[1536]{0:T(1024)} %param.7) | copy-start | bytes 18436
  194.5 2.3 %collective-permute-start.1 = (bf16[97,768]{1,0:T(8,128)(2,1)S(1)}, bf16[97,768]{1,0:T(8,128)(2,1)S(1)}, u32[]{:S(2)}, u32[]{:S(2)}) collective-permute-start(bf16[97,768]{1,0:T(8,128)(2,1)S(1)} %slice.30), channel_id=1, source_target_pairs={{0,1},{2,3},{4,5},{6,7},{8,9},{10,11},{12,13},{14,15},{16,17},{18,... | collective-permute-start | bytes 446984 | tf_op jit(solution)/shard_map/ppermute | solution.py:14
  196.9 3.1 %copy-start.2 = (f32[97,768]{1,0:T(8,128)}, f32[97,768]{1,0:T(8,128)S(1)}, u32[]{:S(2)}) copy-start(f32[97,768]{1,0:T(8,128)S(1)} %fusion.8) | copy-start | bytes 893956
Sparse Core Ops, SparseCore 0:
  46.8 112.0 all-reduce.7
